TPU v7x, 512 devices: a whole 4x4x16 slice. The times are simulated.
512 devices in a mesh: row: 32 (over y, z_hi, core), col: 16 (over z_lo, x).
Axes of the slice: x: 4, y: 4, z: 16 (z_hi: 4, z_lo: 4; z = z_hi * 4 + z_lo), core: 2. Of those that a mesh axis runs over, the one named last changes fastest.
Arguments:
- forcing_terms: float32 [32, 16, 2, 32, 128], P('row', 'col'), may hold values from -6 to 6
- diagonal_reciprocal: float32 [32, 16, 2, 128, 128], P('row', 'col'), may hold values from -0.5 to 0.5
- stiffness_submatrix: float32 [32, 16, 32, 128, 128], P('row', 'col'), may hold values from -0.1875 to 0.1875
- stiffness_source_index: int32 [32, 16, 32], P('row', 'col'), may hold values from 0 to 31
- stiffness_target_index: int32 [32, 16, 32], P('row', 'col'), may hold values from 0 to 63
- stiffness_nonzero_tally: int32 [32, 16], P('row', 'col'), may hold values from 1 to 32, as said below
- interpolant_submatrix: float32 [32, 16, 16, 128, 128], P('row', 'col'), may hold values from -0.0625 to 0.0625
- interpolant_cluster_index: int32 [32, 16, 16], P('row', 'col'), may hold values from 0 to 1
- interpolant_target_index: int32 [32, 16, 16], P('row', 'col'), may hold values from 0 to 63
- interpolant_nonzero_tally: int32 [32, 16], P('row', 'col'), may hold values from 1 to 16, as said below
- provisional_interpolant: float32 [32, 16, 2, 128], P('row', 'col'), may hold values from 0.2 to 1
- cluster_label: int32 [32, 16, 2, 128], P('row', 'col'), may hold values from 0 to 255
Outputs:
- relaxed_iterate: float32 [32, 16, 2, 32, 128], P('row', 'col')
- residual: float32 [32, 16, 2, 32, 128], P('row', 'col')
- coarse: float32 [32, 2, 32, 128], P('row')
Inputs may be any that keep to these rules, and one draw needn't show every extreme that they name: `stiffness_nonzero_tally`: tile slots at or past the count are unused; some pair has all 32 slots live in every draw. `interpolant_nonzero_tally`: tile slots at or past the count are unused; some pair has all 16 slots live in every draw.
All inputs are finite; a program needn't handle non-finite values.
Results may differ from a plain program's by a relative error of at most 0.0003.
Values sent between devices are 32-bit elements; how exact they have to be, the bound alone decides.
No kernel may reach another device: no remote copies, remote signals or barrier semaphores. Data moves between devices by JAX's collectives and lax.ppermute only.
A program may use at most 64 MiB of HBM per device.

v0:
```python
import jax
import jax.numpy as jnp
from jax import lax
from jax.sharding import PartitionSpec as P

omega = 0.7
highest = lax.Precision.HIGHEST
tile_group = 8


def loop_tiles(blocks, stiffness_submatrices, rows, cols, low, high, nout):
    nrhs = blocks.shape[1]
    width = blocks.shape[2]

    def add_group(index, total):
        start = index * tile_group
        piece = lax.dynamic_slice_in_dim(stiffness_submatrices, start, tile_group, 0)
        row_ids = lax.dynamic_slice_in_dim(rows, start, tile_group, 0)
        col_ids = lax.dynamic_slice_in_dim(cols, start, tile_group, 0)
        slots = start + jnp.arange(tile_group)
        live = ((slots >= low) & (slots < high)).astype(jnp.float32)
        inputs = jnp.take(blocks, col_ids, axis=0)
        product = jnp.einsum("ska,sab->skb", inputs, piece, precision=highest)
        onehot = (row_ids[:, None] == jnp.arange(nout)[None, :]).astype(jnp.float32) * live[:, None]
        return total + jnp.einsum("so,skb->okb", onehot, product, precision=highest)

    starting_guess = low // tile_group
    last = (high + tile_group - 1) // tile_group
    empty = jnp.zeros((nout, nrhs, width), jnp.float32)
    return lax.fori_loop(starting_guess, last, add_group, empty)


def gather_columns(vec):
    whole = lax.all_gather(vec[None, None], "row", axis=0, tiled=True)
    return whole.reshape(-1, vec.shape[1], vec.shape[2])


def precondition(vec, inverse):
    return jnp.einsum("pka,pab->pkb", vec, inverse, precision=highest)


def stiffness_product(vec, stiffness_submatrices, rows, cols, count):
    blocks = gather_columns(vec)
    ncol = lax.axis_size("col")
    pblocks = vec.shape[0]
    nout = ncol * pblocks
    partial_value = loop_tiles(blocks, stiffness_submatrices, rows, cols, jnp.int32(0), count, nout)
    partial_value = partial_value.reshape(1, ncol, pblocks, vec.shape[1], vec.shape[2])
    summed = lax.psum_scatter(partial_value, "col", scatter_dimension=1, tiled=True)
    return summed[0, 0]


def body(
    forcing_terms,
    diagonal_reciprocal,
    stiffness_submatrix,
    stiffness_source_index,
    stiffness_target_index,
    stiffness_nonzero_tally,
    interpolant_submatrix,
    interpolant_cluster_index,
    interpolant_target_index,
    interpolant_nonzero_tally,
    provisional_interpolant,
    cluster_label,
):
    source = forcing_terms[0, 0]
    inverse = diagonal_reciprocal[0, 0]
    stiffness_submatrices = stiffness_submatrix[0, 0]
    rows = stiffness_source_index[0, 0]
    cols = stiffness_target_index[0, 0]
    count = stiffness_nonzero_tally[0, 0]
    starting_guess = omega * precondition(source, inverse)
    image_field = stiffness_product(starting_guess, stiffness_submatrices, rows, cols, count)
    relaxed_iterate = starting_guess + omega * precondition(source - image_field, inverse)
    image_field = stiffness_product(relaxed_iterate, stiffness_submatrices, rows, cols, count)
    residual = source - image_field
    pblocks, nrhs, width = residual.shape
    blocks = gather_columns(residual)
    part = loop_tiles(
        blocks,
        interpolant_submatrix[0, 0],
        interpolant_cluster_index[0, 0],
        interpolant_target_index[0, 0],
        jnp.int32(0),
        interpolant_nonzero_tally[0, 0],
        pblocks,
    )
    weighted = (
        (residual * provisional_interpolant[0, 0][:, None, :])
        .transpose(1, 0, 2)
        .reshape(nrhs, pblocks * width)
    )
    onehot = (
        cluster_label[0, 0].reshape(-1)[:, None] == jnp.arange(pblocks * width)[None, :]
    ).astype(jnp.float32)
    tentative = jnp.dot(weighted, onehot, precision=highest)
    part = part + tentative.reshape(nrhs, pblocks, width).transpose(1, 0, 2)
    coarse = lax.psum(part, "col")
    return (relaxed_iterate[None, None], residual[None, None], coarse[None])


def solution(mesh):
    placed = (
        P("row", "col", None, None, None),
        P("row", "col", None, None, None),
        P("row", "col", None, None, None),
        P("row", "col", None),
        P("row", "col", None),
        P("row", "col"),
        P("row", "col", None, None, None),
        P("row", "col", None),
        P("row", "col", None),
        P("row", "col"),
        P("row", "col", None, None),
        P("row", "col", None, None),
    )
    return jax.shard_map(
        body,
        mesh=mesh,
        in_specs=placed,
        out_specs=(
            P("row", "col", None, None, None),
            P("row", "col", None, None, None),
            P("row", None, None, None),
        ),
        check_vma=False,
    )
```

profile of v0, /device:TPU:8, one launch (start us, length us, event | category | flops | bytes accessed | tf_op | source)
XLA Modules:
  0.0 539.8 jit_solution(16684769150870673594)
XLA Ops:
  7.2 0.0 copy-start
  7.2 0.0 all-gather.8.cloned.1.call-start
  7.2 0.8 copy-done
  8.1 1.6 convolution_multiply_fusion.1
  9.7 0.0 all-gather.8.cloned.1.call-update
  9.7 0.0 reduce-scatter.3.cloned.1.call-start
  10.4 76.2 %all-gather.8.cloned.1.call-done = f32[64,32,128]{2,1,0:T(8,128)} async-done(((f32[2,32,128]{2,1,0:T(8,128)}), f32[64,32,128]{2,1,0:T(8,128)}) %all-gather.8.cloned.1.call-update) | async-done | bytes 1048592 | tf_op jit(solution)/shard_map/all_gather | solution.py:34
  86.7 0.0 copy-start.3
  86.7 19.1 %while.30 = (s32[]{:T(128)}, f32[32,32,128]{2,0,1:T(8,128)S(1)}, s32[]{:T(128)}, s32[32]{0:T(128)}, s32[]{:T(128)}, /*index=5*/s32[32]{0:T(128)}, f32[64,32,128]...) while((s32[]{:T(128)}, f32[32,32,128]{2,0,1:T(8,128)S(1)}, ...), condition=%wide.region_1.3_spmd, body=%wide.region_0.2_spmd.sunk | while | flops 63080028 | bytes 2232807 | solution.py:30
  86.7 1.4 compare_and_fusion.6
  88.1 1.8 gather_fusion
  89.9 1.7 fusion.75
  91.6 0.7 dynamic_slice.46
  92.3 0.8 convolution_add_fusion.6
  93.1 1.4 compare_and_fusion.6
  94.5 1.8 gather_fusion
  96.3 1.7 fusion.75
  97.9 0.7 dynamic_slice.46
  98.7 0.8 convolution_add_fusion.6
  99.5 1.4 compare_and_fusion.6
  100.9 1.8 gather_fusion
  102.7 1.7 fusion.75
  104.3 0.7 dynamic_slice.46
  105.0 0.8 convolution_add_fusion.6
  105.9 1.1 copy.25
  107.0 0.0 reduce-scatter.3.cloned.1.call-update
  107.0 0.0 all-gather.10.cloned.1.call-start
  107.1 91.7 %reduce-scatter.3.cloned.1.call-done = f32[1,1,2,32,128]{4,3,2,1,0:T(8,128)} async-done(((f32[1,16,2,32,128]{4,3,2,1,0:T(8,128)}), f32[1,1,2,32,128]{4,3,2,1,0:T(8,128)}) %reduce-scatter.3.cloned.1.call-update) | async-done | bytes 32784 | tf_op jit(solution)/shard_map/reduce_scatter | solution.py:49
  198.8 1.6 fusion.45
  200.4 0.0 all-gather.10.cloned.1.call-update
  200.4 0.0 reduce-scatter.5.cloned.1.call-start
  200.5 68.7 %all-gather.10.cloned.1.call-done = f32[64,32,128]{2,1,0:T(8,128)} async-done(((f32[2,32,128]{2,1,0:T(8,128)}), f32[64,32,128]{2,1,0:T(8,128)}) %all-gather.10.cloned.1.call-update) | async-done | bytes 1048592 | tf_op jit(solution)/shard_map/all_gather | solution.py:34
  269.3 15.3 %while.31 = (s32[]{:T(128)}, f32[32,32,128]{2,0,1:T(8,128)S(1)}, s32[]{:T(128)}, s32[32]{0:T(128)S(1)}, s32[]{:T(128)}, /*index=5*/s32[32]{0:T(128)S(1)}, f32[64...) while((s32[]{:T(128)}, f32[32,32,128]{2,0,1:T(8,128)S(1)}, ...), condition=%wide.region_4.6_spmd, body=%wide.region_3.5_spmd.sunk | while | flops 63080028 | bytes 2232807 | solution.py:30
  269.3 0.8 compare_and_fusion.7
  270.2 1.8 gather_fusion.1
  271.9 1.7 fusion.80
  273.6 0.1 dynamic_slice.48
  273.7 0.8 convolution_add_fusion.7
  274.5 0.7 compare_and_fusion.7
  275.2 1.8 gather_fusion.1
  277.0 1.7 fusion.80
  278.7 0.1 dynamic_slice.48
  278.7 0.8 convolution_add_fusion.7
  279.6 0.7 compare_and_fusion.7
  280.3 1.8 gather_fusion.1
  282.1 1.7 fusion.80
  283.7 0.1 dynamic_slice.48
  283.8 0.8 convolution_add_fusion.7
  284.6 1.1 copy.26
  285.7 0.0 reduce-scatter.5.cloned.1.call-update
  285.8 0.0 all-gather.6.cloned.1.call-start
  285.8 90.4 %reduce-scatter.5.cloned.1.call-done = f32[1,1,2,32,128]{4,3,2,1,0:T(8,128)} async-done(((f32[1,16,2,32,128]{4,3,2,1,0:T(8,128)}), f32[1,1,2,32,128]{4,3,2,1,0:T(8,128)}) %reduce-scatter.5.cloned.1.call-update) | async-done | bytes 32784 | tf_op jit(solution)/shard_map/reduce_scatter | solution.py:49
  376.2 1.4 sub.30
  377.6 0.0 all-gather.6.cloned.1.call-update
  378.3 0.8 fusion.52
  379.2 67.5 %all-gather.6.cloned.1.call-done = f32[32,1,2,32,128]{4,3,2,1,0:T(8,128)} async-done(((f32[1,1,2,32,128]{4,3,2,1,0:T(8,128)}), f32[32,1,2,32,128]{4,3,2,1,0:T(8,128)}) %all-gather.6.cloned.1.call-update) | async-done | bytes 1048592 | tf_op jit(solution)/shard_map/all_gather | solution.py:34
  446.8 3.6 while.32
  446.8 0.7 compare_and_fusion.8
  447.5 1.8 gather_fusion.2
  449.3 0.6 fusion.85
  449.9 0.1 dynamic_slice.50
  450.0 0.3 convolution_add_fusion.8
  450.4 0.3 fusion.44
  450.7 82.6 %psum.7 = f32[1,2,32,128]{3,2,1,0:T(8,128)} all-reduce(f32[1,2,32,128]{3,2,1,0:T(8,128)S(1)} %fusion.44), channel_id=1, replica_groups=mesh['row'=32,'col'=16] {'col'}, use_global_device_ids=true, to_apply=%region_8.10 | all-reduce | flops 8192 | bytes 65536 | tf_op jit(solution)/shard_map/psum | solution.py:99
  (30 shorter events, 0.3 us)
Async XLA Ops:
  7.2 0.9 copy-start
  7.2 79.4 %all-gather.8.cloned.1.call-start = ((), (), s32[]{:S(2)}) async-start(), calls=%async_computation.5 | async-start | bytes 1081344 | tf_op jit(solution)/shard_map/all_gather | solution.py:34
  9.7 189.1 %reduce-scatter.3.cloned.1.call-start = ((), (), s32[]{:S(2)}) async-start(), calls=%async_computation.2 | async-start | bytes 557056 | tf_op jit(solution)/shard_map/reduce_scatter | solution.py:49
  86.7 112.1 %copy-start.2 = (f32[1,1,2,32,128]{4,3,2,1,0:T(8,128)S(1)}, f32[1,1,2,32,128]{4,3,2,1,0:T(8,128)}, u32[]{:S(2)}) copy-start(f32[1,1,2,32,128]{4,3,2,1,0:T(8,128)} %param.20) | copy-start | bytes 98308
  86.7 112.1 %copy-start.3 = (f32[2,32,128]{2,1,0:T(8,128)S(1)}, f32[2,32,128]{2,1,0:T(8,128)}, u32[]{:S(2)}) copy-start(f32[2,32,128]{2,1,0:T(8,128)} %convolution_multiply_fusion.1) | copy-start | bytes 98308
  105.8 163.4 %copy-start.4 = (s32[32]{0:T(128)S(1)}, s32[32]{0:T(128)}, u32[]{:S(2)}) copy-start(s32[32]{0:T(128)} %get-tuple-element.489) | copy-start | bytes 388
  105.9 163.4 %copy-start.8 = (s32[32]{0:T(128)S(1)}, s32[32]{0:T(128)}, u32[]{:S(2)}) copy-start(s32[32]{0:T(128)} %get-tuple-element.491) | copy-start | bytes 388
  107.0 162.2 %all-gather.10.cloned.1.call-start = ((), (), s32[]{:S(2)}) async-start(), calls=%async_computation.6 | async-start | bytes 1081344 | tf_op jit(solution)/shard_map/all_gather | solution.py:34
  200.4 175.8 %reduce-scatter.5.cloned.1.call-start = ((), (), s32[]{:S(2)}) async-start(), calls=%async_computation.3 | async-start | bytes 557056 | tf_op jit(solution)/shard_map/reduce_scatter | solution.py:49
  269.3 109.0 %copy-start.6 = (f32[1,1,2,128]{3,2,1,0:T(2,128)S(1)}, f32[1,1,2,128]{3,2,1,0:T(2,128)}, u32[]{:S(2)}) copy-start(f32[1,1,2,128]{3,2,1,0:T(2,128)} %param.30) | copy-start | bytes 3076
  269.3 177.4 %copy-start.1 = (f32[1,1,16,128,128]{4,3,2,1,0:T(8,128)S(1)}, f32[1,1,16,128,128]{4,3,2,1,0:T(8,128)}, u32[]{:S(2)}) copy-start(f32[1,1,16,128,128]{4,3,2,1,0:T(8,128)} %param.26) | copy-start | bytes 3145732
  269.3 177.4 %copy-start.5 = (s32[1,1,16]{2,1,0:T(1,128)S(1)}, s32[1,1,16]{2,1,0:T(1,128)}, u32[]{:S(2)}) copy-start(s32[1,1,16]{2,1,0:T(1,128)} %param.28) | copy-start | bytes 196
  269.3 177.4 %copy-start.9 = (s32[1,1,16]{2,1,0:T(1,128)S(1)}, s32[1,1,16]{2,1,0:T(1,128)}, u32[]{:S(2)}) copy-start(s32[1,1,16]{2,1,0:T(1,128)} %param.27) | copy-start | bytes 196
  285.8 160.9 %all-gather.6.cloned.1.call-start = ((), (), s32[]{:S(2)}) async-start(), calls=%async_computation.4 | async-start | bytes 1081344 | tf_op jit(solution)/shard_map/all_gather | solution.py:34
  446.7 3.6 copy-start.7
Sparse Core Ops, SparseCore 0:
  11.7 74.8 all-gather.7
  107.1 91.6 reduce-scatter.2
  202.5 66.6 all-gather.9
  285.9 90.2 reduce-scatter.4
  379.8 66.8 all-gather.5
where the time goes:
time: 541 us; the launch traced here: 540 us
  waiting for transfers between devices  395 us (73%)
  blocking collectives  82.6 us (15%)
  matrix products  19.1 us (4%)
  local copies, waits for them, and re-layouts  18.2 us (3%)
  between operations  15.3 us (3%)
  other arithmetic  9.33 us (2%)
    all_gather x3, waiting for transfers between devices, gather_columns(): whole = lax.all_gather(vec[None, None], 'row', axis=0, tiled=True)  212 us
    reduce_scatter x2, waiting for transfers between devices, stiffness_product(): lax.psum_scatter(partial_value, 'col', scatter_dimension=1, tiled=True)  182 us
    psum x1, blocking collectives, body(): coarse = lax.psum(part, 'col')  82.6 us
    gather x7, local copies, waits for them, and re-layouts, add_group(): inputs = jnp.take(blocks, col_ids, axis=0)  12.5 us
  transfers between devices with their start and end apart: 5, of which 5 were waited for; matrix products, arithmetic and copies ran while one was open for 0% of the time, Pallas kernels for 0%

commit v1 on v0

--- a/solution.py
+++ b/solution.py
@@ -31,7 +31,9 @@
 
 
 def gather_columns(vec):
-    whole = lax.all_gather(vec[None, None], "row", axis=0, tiled=True)
+    whole = jnp.concatenate(
+        lax.all_to_all(jnp.stack([vec[None, None]] * lax.axis_size("row")), "row", 0, 0), axis=0
+    )
     return whole.reshape(-1, vec.shape[1], vec.shape[2])
 
 

time: 541 us -> 496 us (0.917)
  the two profiles are of different devices: /device:TPU:8 before, /device:TPU:128 now
where the time goes in v1:
time: 496 us; the launch traced here: 495 us
  waiting for transfers between devices  317 us (64%)
  blocking collectives  82.2 us (17%)
  starting transfers between devices  41.2 us (8%)
  local copies, waits for them, and re-layouts  20.4 us (4%)
  between operations  15.6 us (3%)
  matrix products  11.6 us (2%)
  other arithmetic  5.99 us (1%)
    reduce_scatter x2, waiting for transfers between devices, stiffness_product(): lax.psum_scatter(partial_value, 'col', scatter_dimension=1, tiled=True)  183 us
    all_to_all x3, waiting for transfers between devices, gather_columns(): lax.all_to_all(jnp.stack([vec[None, None]] * lax.axis_size('row')), 'row'...  134 us
    psum x1, blocking collectives, body(): coarse = lax.psum(part, 'col')  82.2 us
    all_to_all x3, starting transfers between devices, gather_columns(): lax.all_to_all(jnp.stack([vec[None, None]] * lax.axis_size('row')), 'row'...  41.1 us
    gather x7, local copies, waits for them, and re-layouts, add_group(): inputs = jnp.take(blocks, col_ids, axis=0)  11.2 us
  transfers between devices with their start and end apart: 5, of which 5 were waited for; matrix products, arithmetic and copies ran while one was open for 0% of the time, Pallas kernels for 0%

profile of v1, /device:TPU:128, one launch (start us, length us, event | category | flops | bytes accessed | tf_op | source)
XLA Modules:
  0.0 494.8 jit_solution(5748546671955443597)
XLA Ops:
  7.2 0.0 copy-start
  7.2 0.9 copy-done
  8.1 1.0 convolution_multiply_fusion.1
  9.1 1.1 stack.9
  10.2 16.6 %all-to-all-start = ((f32[32,1,1,2,32,128]{5,4,3,2,1,0:T(8,128)}), f32[32,1,1,2,32,128]{5,4,3,2,1,0:T(8,128)S(1)}, u32[]{:S(2)}, u32[]{:S(2)}) async-start(f32[32,1,1,2,32,128]{5,4,3,2,1,0:T(8,128)} %stack.9), calls=%async_computation | async-start | bytes 2097152 | tf_op jit(solution)/shard_map/all_to_all | solution.py:35
  26.8 0.0 reduce-scatter.3.cloned.1.call-start
  27.5 49.8 %all-to-all-done = f32[32,1,1,2,32,128]{5,4,3,2,1,0:T(8,128)S(1)} async-done(((f32[32,1,1,2,32,128]{5,4,3,2,1,0:T(8,128)}), f32[32,1,1,2,32,128]{5,4,3,2,1,0:T(8,128)S(1)}, u32[]{:S(2)}, u32[]{:S(2)}) %all-to-all-start) | async-done | bytes 1048608 | tf_op jit(solution)/shard_map/all_to_all | solution.py:35
  77.4 1.0 copy-done.3
  78.4 12.1 %while.30 = (s32[]{:T(128)}, f32[32,32,128]{2,0,1:T(8,128)S(1)}, s32[]{:T(128)}, s32[32]{0:T(128)S(1)}, s32[]{:T(128)}, /*index=5*/s32[32]{0:T(128)S(1)}, f32[64...) while((s32[]{:T(128)}, f32[32,32,128]{2,0,1:T(8,128)S(1)}, ...), condition=%wide.region_1.3_spmd, body=%wide.region_0.2_spmd.sunk | while | flops 63080028 | bytes 2233311 | solution.py:30
  78.5 0.7 compare_and_fusion.6
  79.2 1.8 gather_fusion
  81.0 0.6 fusion.75
  81.6 0.1 dynamic_slice.46
  81.7 0.8 convolution_add_fusion.6
  82.5 0.7 compare_and_fusion.6
  83.2 1.8 gather_fusion
  85.0 0.6 fusion.75
  85.6 0.1 dynamic_slice.46
  85.7 0.8 convolution_add_fusion.6
  86.5 0.7 compare_and_fusion.6
  87.3 1.8 gather_fusion
  89.0 0.6 fusion.75
  89.7 0.1 dynamic_slice.46
  89.7 0.8 convolution_add_fusion.6
  90.5 1.1 copy.25
  91.6 0.0 reduce-scatter.3.cloned.1.call-update
  91.7 91.2 %reduce-scatter.3.cloned.1.call-done = f32[1,1,2,32,128]{4,3,2,1,0:T(8,128)} async-done(((f32[1,16,2,32,128]{4,3,2,1,0:T(8,128)}), f32[1,1,2,32,128]{4,3,2,1,0:T(8,128)}) %reduce-scatter.3.cloned.1.call-update) | async-done | bytes 32784 | tf_op jit(solution)/shard_map/reduce_scatter | solution.py:51
  182.9 1.0 fusion.45
  183.9 1.1 stack.10
  185.0 12.2 %all-to-all-start.1 = ((f32[32,1,1,2,32,128]{5,4,3,2,1,0:T(8,128)}), f32[32,1,1,2,32,128]{5,4,3,2,1,0:T(8,128)S(1)}, u32[]{:S(2)}, u32[]{:S(2)}) async-start(f32[32,1,1,2,32,128]{5,4,3,2,1,0:T(8,128)} %stack.10), calls=%async_computation.2 | async-start | bytes 2097152 | tf_op jit(solution)/shard_map/all_to_all | solution.py:35
  197.3 0.0 reduce-scatter.5.cloned.1.call-start
  197.3 42.5 %all-to-all-done.1 = f32[32,1,1,2,32,128]{5,4,3,2,1,0:T(8,128)S(1)} async-done(((f32[32,1,1,2,32,128]{5,4,3,2,1,0:T(8,128)}), f32[32,1,1,2,32,128]{5,4,3,2,1,0:T(8,128)S(1)}, u32[]{:S(2)}, u32[]{:S(2)}) %all-to-all-start.1) | async-done | bytes 1048608 | tf_op jit(solution)/shard_map/all_to_all | solution.py:35
  239.8 1.0 copy-done.4
  240.8 12.1 %while.31 = (s32[]{:T(128)}, f32[32,32,128]{2,0,1:T(8,128)S(1)}, s32[]{:T(128)}, s32[32]{0:T(128)S(1)}, s32[]{:T(128)}, /*index=5*/s32[32]{0:T(128)S(1)}, f32[64...) while((s32[]{:T(128)}, f32[32,32,128]{2,0,1:T(8,128)S(1)}, ...), condition=%wide.region_4.6_spmd, body=%wide.region_3.5_spmd.sunk | while | flops 63080028 | bytes 2233311 | solution.py:30
  240.9 0.7 compare_and_fusion.7
  241.6 1.8 gather_fusion.1
  243.4 0.6 fusion.80
  244.0 0.1 dynamic_slice.48
  244.1 0.8 convolution_add_fusion.7
  244.9 0.7 compare_and_fusion.7
  245.6 1.8 gather_fusion.1
  247.4 0.6 fusion.80
  248.0 0.1 dynamic_slice.48
  248.1 0.8 convolution_add_fusion.7
  248.9 0.7 compare_and_fusion.7
  249.6 1.8 gather_fusion.1
  251.4 0.6 fusion.80
  252.0 0.1 dynamic_slice.48
  252.1 0.8 convolution_add_fusion.7
  252.9 1.1 copy.26
  254.1 0.0 reduce-scatter.5.cloned.1.call-update
  254.1 92.2 %reduce-scatter.5.cloned.1.call-done = f32[1,1,2,32,128]{4,3,2,1,0:T(8,128)} async-done(((f32[1,16,2,32,128]{4,3,2,1,0:T(8,128)}), f32[1,1,2,32,128]{4,3,2,1,0:T(8,128)}) %reduce-scatter.5.cloned.1.call-update) | async-done | bytes 32784 | tf_op jit(solution)/shard_map/reduce_scatter | solution.py:51
  346.3 0.8 sub.34
  347.1 1.1 stack.11
  348.2 12.3 %all-to-all-start.2 = ((f32[32,1,1,2,32,128]{5,4,3,2,1,0:T(8,128)}), f32[32,1,1,2,32,128]{5,4,3,2,1,0:T(8,128)S(1)}, u32[]{:S(2)}, u32[]{:S(2)}) async-start(f32[32,1,1,2,32,128]{5,4,3,2,1,0:T(8,128)} %stack.11), calls=%async_computation.4 | async-start | bytes 2097152 | tf_op jit(solution)/shard_map/all_to_all | solution.py:35
  361.3 41.7 %all-to-all-done.2 = f32[32,1,1,2,32,128]{5,4,3,2,1,0:T(8,128)S(1)} async-done(((f32[32,1,1,2,32,128]{5,4,3,2,1,0:T(8,128)}), f32[32,1,1,2,32,128]{5,4,3,2,1,0:T(8,128)S(1)}, u32[]{:S(2)}, u32[]{:S(2)}) %all-to-all-start.2) | async-done | bytes 1048608 | tf_op jit(solution)/shard_map/all_to_all | solution.py:35
  403.1 2.4 while.32
  403.1 0.7 compare_and_fusion.8
  403.9 0.6 gather_fusion.2
  404.4 0.6 fusion.85
  405.0 0.1 dynamic_slice.50
  405.1 0.3 convolution_add_fusion.8
  405.5 0.3 fusion.44
  405.8 82.2 %psum.7 = f32[1,2,32,128]{3,2,1,0:T(8,128)} all-reduce(f32[1,2,32,128]{3,2,1,0:T(8,128)S(1)} %fusion.44), channel_id=1, replica_groups=mesh['row'=32,'col'=16] {'col'}, use_global_device_ids=true, to_apply=%region_8.10 | all-reduce | flops 8192 | bytes 65536 | tf_op jit(solution)/shard_map/psum | solution.py:101
  (40 shorter events, 0.3 us)
Async XLA Ops:
  7.2 0.9 copy-start
  7.2 71.2 %copy-start.13 = (s32[1,1,32]{2,1,0:T(1,128)S(1)}, s32[1,1,32]{2,1,0:T(1,128)}, u32[]{:S(2)}) copy-start(s32[1,1,32]{2,1,0:T(1,128)} %param.23) | copy-start | bytes 388
  7.2 71.2 %copy-start.9 = (s32[1,1,32]{2,1,0:T(1,128)S(1)}, s32[1,1,32]{2,1,0:T(1,128)}, u32[]{:S(2)}) copy-start(s32[1,1,32]{2,1,0:T(1,128)} %param.24) | copy-start | bytes 388
  7.2 71.2 %copy-start.1 = (f32[1,1,32,128,128]{4,3,2,1,0:T(8,128)S(1)}, f32[1,1,32,128,128]{4,3,2,1,0:T(8,128)}, u32[]{:S(2)}) copy-start(f32[1,1,32,128,128]{4,3,2,1,0:T(8,128)} %param.22) | copy-start | bytes 6291460
  10.2 67.2 %all-to-all-start = ((f32[32,1,1,2,32,128]{5,4,3,2,1,0:T(8,128)}), f32[32,1,1,2,32,128]{5,4,3,2,1,0:T(8,128)S(1)}, u32[]{:S(2)}, u32[]{:S(2)}) async-start(f32[32,1,1,2,32,128]{5,4,3,2,1,0:T(8,128)} %stack.9), calls=%async_computation | async-start | bytes 2097152 | tf_op jit(solution)/shard_map/all_to_all | solution.py:35
  26.8 156.1 %reduce-scatter.3.cloned.1.call-start = ((), (), s32[]{:S(2)}) async-start(), calls=%async_computation.5 | async-start | bytes 557056 | tf_op jit(solution)/shard_map/reduce_scatter | solution.py:51
  77.3 1.0 copy-start.3
  78.4 104.5 %copy-start.5 = (f32[1,1,2,32,128]{4,3,2,1,0:T(8,128)S(1)}, f32[1,1,2,32,128]{4,3,2,1,0:T(8,128)}, u32[]{:S(2)}) copy-start(f32[1,1,2,32,128]{4,3,2,1,0:T(8,128)} %param.20) | copy-start | bytes 98308
  183.9 56.9 %copy-start.8 = (f32[2,32,128]{2,1,0:T(8,128)}, f32[2,32,128]{2,1,0:T(8,128)S(1)}, u32[]{:S(2)}) copy-start(f32[2,32,128]{2,1,0:T(8,128)S(1)} %fusion.45) | copy-start | bytes 98308
  185.0 54.7 %all-to-all-start.1 = ((f32[32,1,1,2,32,128]{5,4,3,2,1,0:T(8,128)}), f32[32,1,1,2,32,128]{5,4,3,2,1,0:T(8,128)S(1)}, u32[]{:S(2)}, u32[]{:S(2)}) async-start(f32[32,1,1,2,32,128]{5,4,3,2,1,0:T(8,128)} %stack.10), calls=%async_computation.2 | async-start | bytes 2097152 | tf_op jit(solution)/shard_map/all_to_all | solution.py:35
  197.3 149.0 %reduce-scatter.5.cloned.1.call-start = ((), (), s32[]{:S(2)}) async-start(), calls=%async_computation.6 | async-start | bytes 557056 | tf_op jit(solution)/shard_map/reduce_scatter | solution.py:51
  239.8 1.0 copy-start.4
  254.0 107.2 %copy-start.11 = (f32[1,1,2,128]{3,2,1,0:T(2,128)S(1)}, f32[1,1,2,128]{3,2,1,0:T(2,128)}, u32[]{:S(2)}) copy-start(f32[1,1,2,128]{3,2,1,0:T(2,128)} %param.30) | copy-start | bytes 3076
  254.0 149.0 %copy-start.2 = (f32[1,1,16,128,128]{4,3,2,1,0:T(8,128)S(1)}, f32[1,1,16,128,128]{4,3,2,1,0:T(8,128)}, u32[]{:S(2)}) copy-start(f32[1,1,16,128,128]{4,3,2,1,0:T(8,128)} %param.26) | copy-start | bytes 3145732
  254.0 149.0 %copy-start.10 = (s32[1,1,16]{2,1,0:T(1,128)S(1)}, s32[1,1,16]{2,1,0:T(1,128)}, u32[]{:S(2)}) copy-start(s32[1,1,16]{2,1,0:T(1,128)} %param.28) | copy-start | bytes 196
  254.0 149.0 %copy-start.14 = (s32[1,1,16]{2,1,0:T(1,128)S(1)}, s32[1,1,16]{2,1,0:T(1,128)}, u32[]{:S(2)}) copy-start(s32[1,1,16]{2,1,0:T(1,128)} %param.27) | copy-start | bytes 196
  346.3 14.9 %copy-start.7 = (f32[1,1,2,32,128]{4,3,2,1,0:T(8,128)S(1)}, f32[1,1,2,32,128]{4,3,2,1,0:T(8,128)}, u32[]{:S(2)}) copy-start(f32[1,1,2,32,128]{4,3,2,1,0:T(8,128)} %reduce-scatter.5.cloned.1.call-done) | copy-start | bytes 98308
  347.1 56.0 %copy-start.6 = (f32[1,1,2,32,128]{4,3,2,1,0:T(8,128)}, f32[1,1,2,32,128]{4,3,2,1,0:T(8,128)S(1)}, u32[]{:S(2)}) copy-start(f32[1,1,2,32,128]{4,3,2,1,0:T(8,128)S(1)} %sub.34) | copy-start | bytes 98308
  348.2 54.8 %all-to-all-start.2 = ((f32[32,1,1,2,32,128]{5,4,3,2,1,0:T(8,128)}), f32[32,1,1,2,32,128]{5,4,3,2,1,0:T(8,128)S(1)}, u32[]{:S(2)}, u32[]{:S(2)}) async-start(f32[32,1,1,2,32,128]{5,4,3,2,1,0:T(8,128)} %stack.11), calls=%async_computation.4 | async-start | bytes 2097152 | tf_op jit(solution)/shard_map/all_to_all | solution.py:35
  403.1 2.4 copy-start.12
Sparse Core Ops, SparseCore 0:
  91.8 91.0 reduce-scatter.2
  254.2 92.0 reduce-scatter.4
